TPU v7x, 256 devices: a whole 4x4x8 slice. The times are simulated.
256 devices in a mesh: dp: 32 (over y, x, core), tensor: 8 (over z).
Axes of the slice: x: 4, y: 4, z: 8, core: 2. Of those that a mesh axis runs over, the one named last changes fastest.
Arguments:
- patches: bfloat16 [16384, 1280], P('dp'), may hold values from -6 to 6
- window_ids: int32 [32, 512], P('dp'), may hold values from 0 to 15, never falling along the last dimension, each value on 1 to 64 neighbouring positions
- vit_gain: float32 [1280], replicated, may hold values from 0.5 to 2
- qkv_weight: bfloat16 [3, 1280, 1280], P(None, None, 'tensor'), may hold values from -0.15625 to 0.15625
- out_weight: bfloat16 [1280, 1280], P('tensor'), may hold values from -0.15625 to 0.15625
- merge_gain: float32 [1280], replicated, may hold values from 0.5 to 2
- merger_weight: bfloat16 [5120, 3584], P(None, 'tensor'), may hold values from -0.078125 to 0.078125
- audio: bfloat16 [12288, 3584], P('dp', 'tensor'), may hold values from -6 to 6
- span_lengths: int32 [32, 32], replicated, may hold values from 8 to 32, as said below
- span_time: int32 [32, 32], replicated, may hold values from 0 to 31, each once within a row
- llm_gain: float32 [3584], replicated, may hold values from 0.5 to 2
- gate_weight: bfloat16 [3584, 9472], P('dp', 'tensor'), may hold values from -0.09375 to 0.09375
- up_weight: bfloat16 [3584, 9472], P('dp', 'tensor'), may hold values from -0.09375 to 0.09375
- down_weight: bfloat16 [9472, 3584], P('tensor', 'dp'), may hold values from -0.0625 to 0.0625
Outputs:
- mixed: bfloat16 [16384, 3584], P(('dp', 'tensor'))
Inputs may be any that keep to these rules, and one draw needn't show every extreme that they name: `span_lengths`: every row and every column sums to 512; every row and every column holds the value 32 at least once. `span_time`: each row is a permutation of the owners' numbers. `window_ids`: window numbers never fall along a row; a window holds at most 64 patches.
All inputs are finite; a program needn't handle non-finite values.
Results may differ from a plain program's by a relative error of at most 0.017.
Values may be sent and summed in bfloat16 or wider, within the bound.
No kernel may reach another device: no remote copies, remote signals or barrier semaphores. Data moves between devices by JAX's collectives and lax.ppermute only.
A program may use at most 128 MiB of HBM per device.

v0:
```python
import math
import jax
import jax.numpy as jnp
from jax import lax
from jax.sharding import PartitionSpec as P

D_VIT = 1280
HEAD_VIT = 80
EPSILON = 1e-06


def in_blocks(x, dim, devices):
    before, after = (x.shape[:dim], x.shape[dim + 1 :])
    return jnp.moveaxis(x.reshape(*before, devices, -1, *after), dim, 0)


def sent_and_summed(x, axis, dim):
    parts = in_blocks(x, dim, lax.axis_size(axis))
    arrived = lax.all_to_all(parts, axis, split_axis=0, concat_axis=0, tiled=True)
    return arrived.astype(jnp.float32).sum(axis=0)


def from_everyone(x, axis):
    devices = lax.axis_size(axis)
    return lax.all_to_all(jnp.broadcast_to(x[None], (devices, *x.shape)), axis, 0, 0, tiled=True)


def in_order(parts, dim):
    parts = jnp.moveaxis(parts, 0, dim)
    dims = parts.shape
    return parts.reshape(*dims[:dim], dims[dim] * dims[dim + 1], *dims[dim + 2 :])


def gather_directly(x, axis, dim):
    parts = from_everyone(x, axis)
    return in_order(parts, dim)


def gather_turned(arrays, axis, dims):
    turned = [jnp.moveaxis(a, dim, 0) for a, dim in zip(arrays, dims)]
    widths = [t[0].size for t in turned]
    both = jnp.concatenate([t.reshape(-1, w) for t, w in zip(turned, widths)], axis=1)
    whole = lax.all_gather(both, axis, axis=0, tiled=True)
    parts = jnp.split(whole, [sum(widths[:k]) for k in range(1, len(widths))], axis=1)
    return tuple(
        (
            jnp.moveaxis(b.reshape(-1, *t.shape[1:]), 0, dim)
            for b, t, dim in zip(parts, turned, dims)
        )
    )


def rms_scale(values, gain):
    wide = values.astype(jnp.float32)
    meansq = jnp.mean(wide * wide, axis=-1, keepdims=True)
    return wide * lax.rsqrt(meansq + EPSILON) * gain


def body(
    patches,
    window_ids,
    vit_gain,
    qkv_weight,
    out_weight,
    merge_gain,
    merger_weight,
    audio,
    span_lengths,
    span_time,
    llm_gain,
    gate_weight,
    up_weight,
    down_weight,
):
    patch_count = patches.shape[0]
    heads_here = qkv_weight.shape[2] // HEAD_VIT
    normed = rms_scale(patches, vit_gain).astype(jnp.bfloat16)
    query = jnp.dot(normed, qkv_weight[0], preferred_element_type=jnp.float32).astype(jnp.bfloat16)
    keys = jnp.dot(normed, qkv_weight[1], preferred_element_type=jnp.float32).astype(jnp.bfloat16)
    values = jnp.dot(normed, qkv_weight[2], preferred_element_type=jnp.float32).astype(jnp.bfloat16)
    query = query.reshape(patch_count, heads_here, HEAD_VIT)
    keys = keys.reshape(patch_count, heads_here, HEAD_VIT)
    values = values.reshape(patch_count, heads_here, HEAD_VIT)
    scores = jnp.einsum(
        "phe,qhe->hpq", query, keys, preferred_element_type=jnp.float32
    ) / math.sqrt(HEAD_VIT)
    windows = window_ids[0]
    same = windows[:, None] == windows[None, :]
    scores = jnp.where(same[None], scores, -1e30)
    probs = jax.nn.softmax(scores, axis=-1).astype(jnp.bfloat16)
    context = jnp.einsum("hpq,qhe->phe", probs, values, preferred_element_type=jnp.float32).astype(
        jnp.bfloat16
    )
    context = context.reshape(patch_count, heads_here * HEAD_VIT)
    partial_value = jnp.dot(context, out_weight, preferred_element_type=jnp.float32)
    share = sent_and_summed(partial_value.astype(jnp.bfloat16), "tensor", 0)
    share_rows = share.shape[0]
    own_frames = lax.dynamic_slice_in_dim(
        patches, lax.axis_index("tensor") * share_rows, share_rows, 0
    )
    own_encoded = (own_frames.astype(jnp.float32) + share).astype(jnp.bfloat16)
    encoded = gather_directly(own_encoded, "tensor", 0)
    merged = (
        rms_scale(encoded, merge_gain).astype(jnp.bfloat16).reshape(patch_count // 4, 4 * D_VIT)
    )
    video = jnp.dot(merged, merger_weight, preferred_element_type=jnp.float32).astype(jnp.bfloat16)
    source = jnp.concatenate([video, audio], axis=0)
    seq_count = source.shape[0]
    owner_count = lax.axis_size("dp")
    owner = lax.axis_index("dp")
    capacity = 2 * seq_count // owner_count
    sent_lengths = span_lengths[owner]
    starts = jnp.cumsum(sent_lengths) - sent_lengths
    slot_index = jnp.arange(capacity, dtype=jnp.int32)
    occupied = slot_index[None, :] < sent_lengths[:, None]
    source_index = jnp.where(occupied, starts[:, None] + slot_index[None, :], 0).reshape(-1)
    outgoing = jnp.take(source, source_index, axis=0)
    outgoing = jnp.where(occupied.reshape(-1)[:, None], outgoing, jnp.zeros((), outgoing.dtype))
    incoming = lax.all_to_all(outgoing, "dp", split_axis=0, concat_axis=0, tiled=True)
    taken_lengths = span_lengths[:, owner]
    arrival = span_time[owner]
    earlier = arrival[:, None] < arrival[None, :]
    offsets = jnp.sum(jnp.where(earlier, taken_lengths[:, None], 0), axis=0)
    position = jnp.arange(seq_count, dtype=jnp.int32)
    inside = (position[None, :] >= offsets[:, None]) & (
        position[None, :] < offsets[:, None] + taken_lengths[:, None]
    )
    sender = jnp.arange(owner_count, dtype=jnp.int32)[:, None]
    slot_row = sender * capacity + position[None, :] - offsets[:, None]
    picked = jnp.sum(jnp.where(inside, slot_row, 0), axis=0)
    sequence = jnp.take(incoming, picked, axis=0)
    features = lax.all_gather(sequence, "tensor", axis=1, tiled=True)
    normed_seq = rms_scale(features, llm_gain).astype(jnp.bfloat16)
    gate_full, up_full, down_full = gather_turned(
        (gate_weight, up_weight, down_weight), "dp", (0, 0, 1)
    )
    gate = jnp.dot(normed_seq, gate_full, preferred_element_type=jnp.float32)
    upward = jnp.dot(normed_seq, up_full, preferred_element_type=jnp.float32)
    hidden = (jax.nn.silu(gate) * upward).astype(jnp.bfloat16)
    terms = jnp.dot(hidden, down_full, preferred_element_type=jnp.float32)
    summed = lax.psum_scatter(
        terms.astype(jnp.bfloat16), "tensor", scatter_dimension=0, tiled=True
    ).astype(jnp.float32)
    own_count = summed.shape[0]
    own_rows = lax.dynamic_slice_in_dim(
        features, lax.axis_index("tensor") * own_count, own_count, 0
    )
    return (own_rows.astype(jnp.float32) + summed).astype(jnp.bfloat16)


def solution(mesh):
    return jax.shard_map(
        body,
        mesh=mesh,
        in_specs=(
            P("dp", None),
            P("dp", None),
            P(),
            P(None, None, "tensor"),
            P("tensor", None),
            P(),
            P(None, "tensor"),
            P("dp", "tensor"),
            P(),
            P(),
            P(),
            P("dp", "tensor"),
            P("dp", "tensor"),
            P("tensor", "dp"),
        ),
        out_specs=P(("dp", "tensor"), None),
        check_vma=False,
    )
```

profile of v0, /device:TPU:1, one launch (start us, length us, event | category | flops | bytes accessed | tf_op | source)
XLA Modules:
  0.0 377.8 jit_solution(1047735685525039576)
XLA Ops:
  6.5 1.8 fusion.19
  8.4 2.1 convolution_convert_fusion.3
  10.5 0.7 convolution_convert_fusion.2
  11.1 0.7 convolution_convert_fusion.4
  11.8 0.2 broadcast_compare_fusion
  12.0 1.0 fusion.61
  13.0 1.2 convolution_convert_fusion.1
  14.3 1.6 convolution_convert_fusion
  15.9 9.0 %all-to-all-start = ((bf16[8,64,1280]{2,1,0:T(8,128)(2,1)}), bf16[8,64,1280]{2,1,0:T(8,128)(2,1)S(1)}, u32[]{:S(2)}, u32[]{:S(2)}) async-start(bf16[8,64,1280]{2,1,0:T(8,128)(2,1)} %bitcast.15), calls=%async_computation | async-start | bytes 2621440 | tf_op jit(solution)/shard_map/all_to_all | solution.py:19
  24.9 34.9 %all-to-all-done = bf16[8,64,1280]{2,1,0:T(8,128)(2,1)S(1)} async-done(((bf16[8,64,1280]{2,1,0:T(8,128)(2,1)}), bf16[8,64,1280]{2,1,0:T(8,128)(2,1)S(1)}, u32[]{:S(2)}, u32[]{:S(2)}) %all-to-all-start) | async-done | bytes 1310752 | tf_op jit(solution)/shard_map/all_to_all | solution.py:19
  59.8 0.2 convert_reduce_fusion
  60.1 1.1 broadcast_in_dim.103
  61.2 3.6 all-to-all-start.1
  64.8 0.2 copy.36
  65.1 0.1 copy.33
  65.2 0.1 reduce.1
  65.4 0.1 select_n.94
  65.6 0.1 copy.40
  65.7 0.7 fusion.44
  66.4 0.1 select_reduce_fusion.1
  66.5 0.1 iota_compare_fusion.2
  66.6 32.9 %all-to-all-done.1 = bf16[8,64,1280]{2,1,0:T(8,128)(2,1)S(1)} async-done(((bf16[8,64,1280]{2,1,0:T(8,128)(2,1)}), bf16[8,64,1280]{2,1,0:T(8,128)(2,1)S(1)}, u32[]{:S(2)}, u32[]{:S(2)}) %all-to-all-start.1) | async-done | bytes 1310752 | tf_op jit(solution)/shard_map/all_to_all | solution.py:25
  99.5 0.3 multiply_reduce_fusion
  99.9 0.1 rsqrt.29
  100.0 0.4 mul.97
  100.4 2.0 copy.42
  102.3 1.9 reshape.242
  104.2 5.2 %fusion.25 = bf16[128,448]{0,1:T(8,128)(2,1)S(1)} fusion(bf16[5120,448]{0,1:T(8,128)(2,1)} %param.20, f32[128,5120]{1,0:T(8,128)} %reshape.242, f32[128,5120]{1,0:T(8,128)} %bitcast.49, f32[5120]{0:T(1024)S(1)} %mul.101), kind=kOutput, calls=%fused_computation.36 | convolution fusion | flops 589225984 | bytes 9965568 | tf_op jit(solution)/shard_map/dot_general | solution.py:106
  109.4 0.1 copy.35
  109.6 4.0 %gather_fusion = bf16[1024,448]{1,0:T(8,128)(2,1)S(1)} fusion(bf16[512,448]{1,0:T(8,128)(2,1)S(1)} %pad_maximum_fusion, s32[1024]{0:T(1024)S(1)} %broadcast_clamp_fusion), kind=kCustom, calls=%fused_computation | custom fusion | bytes 1839104 | tf_op jit(solution)/shard_map/jit(_take)/gather | solution.py:117
  113.6 1.3 select_select_fusion
  114.9 7.6 %all-to-all-start.2 = ((bf16[32,32,448]{2,1,0:T(8,128)(2,1)}), bf16[32,32,448]{2,1,0:T(8,128)(2,1)S(1)}, u32[]{:S(2)}, u32[]{:S(2)}) async-start(bf16[32,32,448]{2,1,0:T(8,128)(2,1)} %select_select_fusion), calls=%async_computation.2 | async-start | bytes 2097152 | tf_op jit(solution)/shard_map/all_to_all | solution.py:119
  122.5 0.1 select_reduce_fusion
  122.6 17.0 %all-to-all-done.2 = bf16[32,32,448]{2,1,0:T(8,128)(2,1)S(1)} async-done(((bf16[32,32,448]{2,1,0:T(8,128)(2,1)}), bf16[32,32,448]{2,1,0:T(8,128)(2,1)S(1)}, u32[]{:S(2)}, u32[]{:S(2)}) %all-to-all-start.2) | async-done | bytes 917536 | tf_op jit(solution)/shard_map/all_to_all | solution.py:119
  139.6 2.0 gather_fusion.1
  141.6 0.1 broadcast_select_fusion
  141.7 1.0 copy.37
  142.8 1.4 concatenate.7
  144.2 0.2 reduce-scatter.2.cloned.1.call-start
  144.4 40.7 %all-gather.3.cloned.1.call-done = bf16[512,3584]{0,1:T(8,128)(2,1)} async-done(((bf16[512,448]{0,1:T(8,128)(2,1)}), bf16[512,3584]{0,1:T(8,128)(2,1)}) %all-gather.3.cloned.1.call-update) | async-done | bytes 3670032 | tf_op jit(solution)/shard_map/all_gather | solution.py:132
  185.1 2.9 fusion.7
  188.0 97.1 %all-gather.5.cloned.1.call-done = bf16[3584,3552]{1,0:T(8,128)(2,1)} async-done(((bf16[112,3552]{1,0:T(8,128)(2,1)}), bf16[3584,3552]{1,0:T(8,128)(2,1)}) %all-gather.5.cloned.1.call-update) | async-done | bytes 25460752 | tf_op jit(solution)/shard_map/all_gather | solution.py:43
  285.1 9.8 %fusion.5 = f32[512,1184]{0,1:T(8,128)S(1)} fusion(bf16[3584,3552]{1,0:T(8,128)(2,1)} %all-gather.5.cloned.1.call-done, bf16[512,3584]{0,1:T(8,128)(2,1)} %all-gather.3.cloned.1.call-done, f32[3584]{0:T(1024)S(1)} %copy-done.11, f32[512]{0:T(512)S(1)} %add_rsqrt_fusion.1), kind=kOutput, calls=%fused_computation.7 | convolution fusion | flops 4352638976 | bytes 15286272 | tf_op jit(solution)/shard_map/dot_general | solution.py:137
  294.9 24.9 %fusion.10 = bf16[512,3584]{1,0:T(8,128)(2,1)} fusion(bf16[3584,3552]{1,0:T(8,128)(2,1)} %all-gather.5.cloned.1.call-done, f32[512,1184]{0,1:T(8,128)S(1)} %fusion.5, bf16[512,3584]{0,1:T(8,128)(2,1)} %all-gather.3.cloned.1.call-done, f32[3584]{0:T(1024)S(1)} %copy-done.11, f32[512]{0:T(512)S(1)} %add_rsqrt_fusion.1), kind=kOutput, calls=%fused_computation.14 | convolution fusion | flops 8703410176 | bytes 28131328 | tf_op jit(solution)/shard_map/dot_general | solution.py:140
  319.8 1.6 constant_dynamic-slice_fusion
  321.4 0.3 copy.41
  321.7 47.7 %reduce-scatter.2.cloned.1.call-done = bf16[64,3584]{1,0:T(8,128)(2,1)} async-done(((bf16[512,3584]{1,0:T(8,128)(2,1)}), bf16[64,3584]{1,0:T(8,128)(2,1)}) %reduce-scatter.2.cloned.1.call-update) | async-done | bytes 458768 | tf_op jit(solution)/shard_map/reduce_scatter | solution.py:141
  369.4 1.9 add_convert_fusion
  (50 shorter events, 0.6 us)
Async XLA Ops:
  6.5 7.7 %copy-start = (bf16[160,1280]{1,0:T(8,128)(2,1)S(1)}, bf16[160,1280]{1,0:T(8,128)(2,1)}, u32[]{:S(2)}) copy-start(bf16[160,1280]{1,0:T(8,128)(2,1)} %param.18) | copy-start | bytes 1228804
  6.5 3.9 %copy-start.2 = (bf16[512,1280]{1,0:T(8,128)(2,1)S(1)}, bf16[512,1280]{1,0:T(8,128)(2,1)}, u32[]{:S(2)}) copy-start(bf16[512,1280]{1,0:T(8,128)(2,1)} %param.14) | copy-start | bytes 3932164
  6.5 3.9 %copy-start.12 = (f32[1280]{0:T(1024)S(1)}, f32[1280]{0:T(1024)}, u32[]{:S(2)}) copy-start(f32[1280]{0:T(1024)} %param.16) | copy-start | bytes 15364
  6.5 3.9 %copy-start.10 = (bf16[3,1280,160]{1,2,0:T(8,128)(2,1)S(1)}, bf16[3,1280,160]{1,2,0:T(8,128)(2,1)}, u32[]{:S(2)}) copy-start(bf16[3,1280,160]{1,2,0:T(8,128)(2,1)} %param.17) | copy-start | bytes 3686404
  10.5 1.3 copy-start.8
  15.9 43.9 %all-to-all-start = ((bf16[8,64,1280]{2,1,0:T(8,128)(2,1)}), bf16[8,64,1280]{2,1,0:T(8,128)(2,1)S(1)}, u32[]{:S(2)}, u32[]{:S(2)}) async-start(bf16[8,64,1280]{2,1,0:T(8,128)(2,1)} %bitcast.15), calls=%async_computation | async-start | bytes 2621440 | tf_op jit(solution)/shard_map/all_to_all | solution.py:19
  60.0 4.8 %copy-start.9 = (f32[1280]{0:T(1024)S(1)}, f32[1280]{0:T(1024)}, u32[]{:S(2)}) copy-start(f32[1280]{0:T(1024)} %param.19) | copy-start | bytes 15364
  60.0 4.8 %copy-start.3 = (bf16[384,448]{0,1:T(8,128)(2,1)S(1)}, bf16[384,448]{0,1:T(8,128)(2,1)}, u32[]{:S(2)}) copy-start(bf16[384,448]{0,1:T(8,128)(2,1)} %param.21) | copy-start | bytes 1032196
  60.0 5.0 %copy-start.7 = (s32[32,32]{1,0:T(8,128)S(1)}, s32[32,32]{1,0:T(8,128)}, u32[]{:S(2)}) copy-start(s32[32,32]{1,0:T(8,128)} %param.22) | copy-start | bytes 12292
  61.2 38.3 %all-to-all-start.1 = ((bf16[8,64,1280]{2,1,0:T(8,128)(2,1)}), bf16[8,64,1280]{2,1,0:T(8,128)(2,1)S(1)}, u32[]{:S(2)}, u32[]{:S(2)}) async-start(bf16[8,64,1280]{2,1,0:T(8,128)(2,1)} %broadcast_in_dim.103), calls=%async_computation.1 | async-start | bytes 2621440 | tf_op jit(solution)/shard_map/all_to_all | solution.py:25
  114.9 24.8 %all-to-all-start.2 = ((bf16[32,32,448]{2,1,0:T(8,128)(2,1)}), bf16[32,32,448]{2,1,0:T(8,128)(2,1)S(1)}, u32[]{:S(2)}, u32[]{:S(2)}) async-start(bf16[32,32,448]{2,1,0:T(8,128)(2,1)} %select_select_fusion), calls=%async_computation.2 | async-start | bytes 2097152 | tf_op jit(solution)/shard_map/all_to_all | solution.py:119
  122.4 62.7 %all-gather.3.cloned.1.call-start = ((), (), s32[]{:S(2)}) async-start(), calls=%async_computation.4 | async-start | bytes 4128768 | tf_op jit(solution)/shard_map/all_gather | solution.py:132
  139.6 3.2 copy-start.4
  139.6 3.2 copy-start.5
  139.6 3.2 copy-start.6
  142.7 142.4 %all-gather.5.cloned.1.call-start = ((), (), s32[]{:S(2)}) async-start(), calls=%async_computation.5 | async-start | bytes 26492928 | tf_op jit(solution)/shard_map/all_gather | solution.py:43
  144.1 141.0 %copy-start.11 = (f32[3584]{0:T(1024)S(1)}, f32[3584]{0:T(1024)}, u32[]{:S(2)}) copy-start(f32[3584]{0:T(1024)} %param.24) | copy-start | bytes 43012
  144.2 225.2 %reduce-scatter.2.cloned.1.call-start = ((), (), s32[]{:S(2)}) async-start(), calls=%async_computation.6 | async-start | bytes 4128768 | tf_op jit(solution)/shard_map/reduce_scatter | solution.py:141
  319.8 51.5 %copy-start.1 = (bf16[160,1280]{1,0:T(8,128)(2,1)S(1)}, bf16[160,1280]{1,0:T(8,128)(2,1)}, u32[]{:S(2)}) copy-start(bf16[160,1280]{1,0:T(8,128)(2,1)} %param.18) | copy-start | bytes 1228804
Sparse Core Ops, SparseCore 0:
  142.8 42.2 all-gather.2
  187.7 97.3 all-gather.4
  319.9 49.4 reduce-scatter.1
where the time goes:
time: 378 us
  waiting for transfers between devices  270 us (71%)
  matrix products  47.1 us (12%)
  starting transfers between devices  20.5 us (5%)
  local copies, waits for them, and re-layouts  17 us (4%)
  between operations  13.5 us (4%)
  other arithmetic  9.35 us (2%)
    all_gather x1, waiting for transfers between devices, gather_turned(): whole = lax.all_gather(both, axis, axis=0, tiled=True)  97.1 us
    reduce_scatter x1, waiting for transfers between devices, body(): lax.psum_scatter(terms.astype(jnp.bfloat16), 'tensor', scatter_dimension=...  47.7 us
    all_gather x1, waiting for transfers between devices, body(): features = lax.all_gather(sequence, 'tensor', axis=1, tiled=True)  40.7 us
    all_to_all x1, waiting for transfers between devices, sent_and_summed(): lax.all_to_all(parts, axis, split_axis=0, concat_axis=0, tiled=True)  34.9 us
    all_to_all x1, waiting for transfers between devices, from_everyone(): lax.all_to_all(jnp.broadcast_to(x[None], (devices, *x.shape)), axis, 0, 0...  32.9 us
    dot_general x1, matrix products, body(): terms = jnp.dot(hidden, down_full, preferred_element_type=jnp.float32)  24.9 us
    all_to_all x1, waiting for transfers between devices, body(): lax.all_to_all(outgoing, 'dp', split_axis=0, concat_axis=0, tiled=True)  17 us
    dot_general x1, matrix products, body(): gate = jnp.dot(normed_seq, gate_full, preferred_element_type=jnp.float32)  9.77 us
  transfers between devices with their start and end apart: 6, of which 6 were waited for; matrix products, arithmetic and copies ran while one was open for 2% of the time, Pallas kernels for 0%

commit v1 on v0

--- a/solution.py
+++ b/solution.py
@@ -129,7 +129,16 @@
     slot_row = sender * capacity + position[None, :] - offsets[:, None]
     picked = jnp.sum(jnp.where(inside, slot_row, 0), axis=0)
     sequence = jnp.take(incoming, picked, axis=0)
-    features = lax.all_gather(sequence, "tensor", axis=1, tiled=True)
+    ways = lax.axis_size("tensor")
+    up = [(d, (d + 1) % ways) for d in range(ways)]
+    down = [(d, (d - 1) % ways) for d in range(ways)]
+    earlier_2, later = ([sequence], [sequence])
+    for _ in range(ways // 2):
+        earlier_2.append(lax.ppermute(earlier_2[-1], "tensor", up))
+    for _ in range((ways - 1) // 2):
+        later.append(lax.ppermute(later[-1], "tensor", down))
+    line = jnp.concatenate([*earlier_2[::-1], *later[1:]], axis=1)
+    features = jnp.roll(line, (lax.axis_index("tensor") - ways // 2) * sequence.shape[1], axis=1)
     normed_seq = rms_scale(features, llm_gain).astype(jnp.bfloat16)
     gate_full, up_full, down_full = gather_turned(
         (gate_weight, up_weight, down_weight), "dp", (0, 0, 1)

time: 378 us -> 314 us (0.83)
  waiting for transfers between devices: 270 us -> 178 us
  local copies, waits for them, and re-layouts: 17 us -> 27 us
  starting transfers between devices: 20.5 us -> 28.6 us
  matrix products: 47.1 us -> 54.4 us
    all_gather x1, waiting for transfers between devices: 97.1 us -> 0.02 us  [gather_turned(): whole = lax.all_gather(both, axis, axis=0, tiled=True)]
    ppermute x0 -> x7, waiting for transfers between devices: none -> 43.8 us  [the longest x4 43.8 us: body(): earlier_2.append(lax.ppermute(earlier_2[-1], 'tensor', up))]
    all_gather x1 -> x0, waiting for transfers between devices: 40.7 us -> none  [body(): features = lax.all_gather(sequence, 'tensor', axis=1, tiled=True)]
    dot_general x0 -> x1, matrix products: none -> 14.2 us  [body(): upward = jnp.dot(normed_seq, up_full, preferred_element_type=jnp.float32)]
    concatenate x0 -> x1, local copies, waits for them, and re-layouts: none -> 11.6 us  [body(): jnp.roll(line, (lax.axis_index('tensor') - ways // 2) * sequence.shape[1]...]
    dot_general x1, matrix products: 24.9 us -> 15.8 us  [body(): terms = jnp.dot(hidden, down_full, preferred_element_type=jnp.float32)]
    ppermute x0 -> x7, starting transfers between devices: none -> 8.11 us  [the longest x3 7.73 us: body(): later.append(lax.ppermute(later[-1], 'tensor', down))]
  transfers between devices with their start and end apart: 6 -> 12, of which waited for: 6 -> 8; matrix products, arithmetic and copies ran while one was open for 2% -> 15% of each run, Pallas kernels for 0% -> 0%
where the time goes in v1:
time: 314 us; the launch traced here: 312 us
  waiting for transfers between devices  178 us (57%)
  matrix products  54.4 us (17%)
  starting transfers between devices  28.6 us (9%)
  local copies, waits for them, and re-layouts  27 us (9%)
  between operations  13.8 us (4%)
  other arithmetic  10.5 us (3%)
    reduce_scatter x1, waiting for transfers between devices, body(): lax.psum_scatter(terms.astype(jnp.bfloat16), 'tensor', scatter_dimension=...  49.2 us
    ppermute x4, waiting for transfers between devices, body(): earlier_2.append(lax.ppermute(earlier_2[-1], 'tensor', up))  43.8 us
    all_to_all x1, waiting for transfers between devices, sent_and_summed(): lax.all_to_all(parts, axis, split_axis=0, concat_axis=0, tiled=True)  34.9 us
    all_to_all x1, waiting for transfers between devices, from_everyone(): lax.all_to_all(jnp.broadcast_to(x[None], (devices, *x.shape)), axis, 0, 0...  33 us
    all_to_all x1, waiting for transfers between devices, body(): lax.all_to_all(outgoing, 'dp', split_axis=0, concat_axis=0, tiled=True)  17 us
    dot_general x1, matrix products, body(): terms = jnp.dot(hidden, down_full, preferred_element_type=jnp.float32)  15.8 us
    dot_general x1, matrix products, body(): upward = jnp.dot(normed_seq, up_full, preferred_element_type=jnp.float32)  14.2 us
    concatenate x1, local copies, waits for them, and re-layouts, body(): jnp.roll(line, (lax.axis_index('tensor') - ways // 2) * sequence.shape[1]...  11.6 us
  transfers between devices with their start and end apart: 12, of which 8 were waited for; matrix products, arithmetic and copies ran while one was open for 15% of the time, Pallas kernels for 0%

profile of v1, /device:TPU:1, one launch (start us, length us, event | category | flops | bytes accessed | tf_op | source)
XLA Modules:
  0.0 312.2 jit_solution(475434443989635854)
XLA Ops:
  6.6 2.4 concatenate.14
  9.0 0.3 fusion.13
  9.4 0.2 broadcast_compare_fusion
  9.6 1.7 convolution_convert_fusion.3
  11.3 1.7 convolution_convert_fusion.2
  12.9 1.0 fusion.54
  13.9 1.7 convolution_convert_fusion.4
  15.6 1.2 convolution_convert_fusion.1
  16.9 1.7 convolution_convert_fusion
  18.5 9.0 %all-to-all-start = ((bf16[8,64,1280]{2,1,0:T(8,128)(2,1)}), bf16[8,64,1280]{2,1,0:T(8,128)(2,1)S(1)}, u32[]{:S(2)}, u32[]{:S(2)}) async-start(bf16[8,64,1280]{2,1,0:T(8,128)(2,1)} %bitcast.15), calls=%async_computation | async-start | bytes 2621440 | tf_op jit(solution)/shard_map/all_to_all | solution.py:19
  27.5 34.9 %all-to-all-done = bf16[8,64,1280]{2,1,0:T(8,128)(2,1)S(1)} async-done(((bf16[8,64,1280]{2,1,0:T(8,128)(2,1)}), bf16[8,64,1280]{2,1,0:T(8,128)(2,1)S(1)}, u32[]{:S(2)}, u32[]{:S(2)}) %all-to-all-start) | async-done | bytes 1310752 | tf_op jit(solution)/shard_map/all_to_all | solution.py:19
  62.4 0.2 convert_reduce_fusion
  62.7 1.2 broadcast_in_dim.103
  63.9 3.6 %all-to-all-start.1 = ((bf16[8,64,1280]{2,1,0:T(8,128)(2,1)}), bf16[8,64,1280]{2,1,0:T(8,128)(2,1)S(1)}, u32[]{:S(2)}, u32[]{:S(2)}) async-start(bf16[8,64,1280]{2,1,0:T(8,128)(2,1)} %broadcast_in_dim.103), calls=%async_computation.1 | async-start | bytes 2621440 | tf_op jit(solution)/shard_map/all_to_all | solution.py:25
  67.6 0.1 reduce.1
  68.1 0.2 copy.29
  68.3 0.7 fusion.37
  69.0 0.1 select_reduce_fusion.1
  69.2 33.0 %all-to-all-done.1 = bf16[8,64,1280]{2,1,0:T(8,128)(2,1)S(1)} async-done(((bf16[8,64,1280]{2,1,0:T(8,128)(2,1)}), bf16[8,64,1280]{2,1,0:T(8,128)(2,1)S(1)}, u32[]{:S(2)}, u32[]{:S(2)}) %all-to-all-start.1) | async-done | bytes 1310752 | tf_op jit(solution)/shard_map/all_to_all | solution.py:25
  102.2 0.3 multiply_reduce_fusion
  102.5 0.1 rsqrt.29
  102.6 0.4 mul.100
  103.0 2.0 copy.32
  105.1 1.9 reshape.242
  107.0 5.2 %fusion.20 = bf16[128,448]{0,1:T(8,128)(2,1)S(1)} fusion(bf16[5120,448]{0,1:T(8,128)(2,1)} %param.20, f32[128,5120]{1,0:T(8,128)} %reshape.242, f32[128,5120]{1,0:T(8,128)} %bitcast.49, f32[5120]{0:T(1024)S(1)} %mul.104), kind=kOutput, calls=%fused_computation.36 | convolution fusion | flops 589225984 | bytes 9965568 | tf_op jit(solution)/shard_map/dot_general | solution.py:106
  112.2 0.1 copy.28
  112.4 4.0 %gather_fusion = bf16[1024,448]{1,0:T(8,128)(2,1)S(1)} fusion(bf16[512,448]{1,0:T(8,128)(2,1)S(1)} %pad_maximum_fusion, s32[1024]{0:T(1024)S(1)} %broadcast_clamp_fusion), kind=kCustom, calls=%fused_computation | custom fusion | bytes 1839104 | tf_op jit(solution)/shard_map/jit(_take)/gather | solution.py:117
  116.4 1.3 select_select_fusion
  117.6 7.8 %all-to-all-start.2 = ((bf16[32,32,448]{2,1,0:T(8,128)(2,1)}), bf16[32,32,448]{2,1,0:T(8,128)(2,1)S(1)}, u32[]{:S(2)}, u32[]{:S(2)}) async-start(bf16[32,32,448]{2,1,0:T(8,128)(2,1)} %select_select_fusion), calls=%async_computation.2 | async-start | bytes 2097152 | tf_op jit(solution)/shard_map/all_to_all | solution.py:119
  125.5 0.1 select_reduce_fusion
  125.7 17.0 %all-to-all-done.2 = bf16[32,32,448]{2,1,0:T(8,128)(2,1)S(1)} async-done(((bf16[32,32,448]{2,1,0:T(8,128)(2,1)}), bf16[32,32,448]{2,1,0:T(8,128)(2,1)S(1)}, u32[]{:S(2)}, u32[]{:S(2)}) %all-to-all-start.2) | async-done | bytes 917536 | tf_op jit(solution)/shard_map/all_to_all | solution.py:119
  142.7 2.0 gather_fusion.1
  144.6 0.1 broadcast_select_fusion
  144.8 0.4 collective-permute-start
  145.1 2.4 collective-permute-start.4
  147.5 11.6 %collective-permute-done = bf16[512,448]{1,0:T(8,128)(2,1)S(1)} collective-permute-done((bf16[512,448]{1,0:T(8,128)(2,1)S(1)}, bf16[512,448]{1,0:T(8,128)(2,1)S(1)}, u32[]{:S(2)}, u32[]{:S(2)}) %collective-permute-start) | collective-permute-done | bytes 458784 | tf_op jit(solution)/shard_map/ppermute | solution.py:137
  159.2 2.7 collective-permute-start.5
  161.9 10.7 %collective-permute-done.1 = bf16[512,448]{1,0:T(8,128)(2,1)S(1)} collective-permute-done((bf16[512,448]{1,0:T(8,128)(2,1)S(1)}, bf16[512,448]{1,0:T(8,128)(2,1)S(1)}, u32[]{:S(2)}, u32[]{:S(2)}) %collective-permute-start.1) | collective-permute-done | bytes 458784 | tf_op jit(solution)/shard_map/ppermute | solution.py:137
  172.6 2.7 collective-permute-start.6
  175.3 9.8 %collective-permute-done.2 = bf16[512,448]{1,0:T(8,128)(2,1)S(1)} collective-permute-done((bf16[512,448]{1,0:T(8,128)(2,1)S(1)}, bf16[512,448]{1,0:T(8,128)(2,1)S(1)}, u32[]{:S(2)}, u32[]{:S(2)}) %collective-permute-start.2) | collective-permute-done | bytes 458784 | tf_op jit(solution)/shard_map/ppermute | solution.py:137
  185.1 11.7 %collective-permute-done.3 = bf16[512,448]{1,0:T(8,128)(2,1)} collective-permute-done((bf16[512,448]{1,0:T(8,128)(2,1)S(1)}, bf16[512,448]{1,0:T(8,128)(2,1)}, u32[]{:S(2)}, u32[]{:S(2)}) %collective-permute-start.3) | collective-permute-done | bytes 458784 | tf_op jit(solution)/shard_map/ppermute | solution.py:137
  196.7 11.6 %concatenate.13 = bf16[512,7168]{1,0:T(8,128)(2,1)} concatenate(bf16[512,448]{1,0:T(8,128)(2,1)} %collective-permute-done.3, bf16[512,448]{1,0:T(8,128)(2,1)S(1)} %collective-permute-done.2, bf16[512,448]{1,0:T(8,128)(2,1)S(1)} %collective-permute-done.1, bf16[512,448]{1,0:T(8,128)(2,1)S(1)} %collective-permute-done, bf16[512,448]{1,0:T(8,128)(2,1)S(1)} %broadcast_select_fusion, ...), dimensions={1} | concatenate | bytes 14680064 | tf_op jit(solution)/shard_map/jit(_roll_dynamic)/concatenate | solution.py:141
  208.4 5.2 %fusion.7 = f32[512]{0:T(512)S(1)} fusion(bf16[512,7168]{1,0:T(8,128)(2,1)} %concatenate.13, s32[]{:T(128)S(6)} %select_n.119), kind=kLoop, calls=%fused_computation.11 | loop fusion | flops 5504512 | bytes 3672068 | tf_op jit(solution)/shard_map/reduce_sum | solution.py:55
  213.6 14.2 %fusion.3 = f32[512,1184]{0,1:T(8,128)S(1)} fusion(bf16[3584,3552]{1,0:T(8,128)(2,1)} %all-gather.2.cloned.1.call-done, f32[3584]{0:T(1024)S(1)} %copy-done.7, f32[512]{0:T(512)S(1)} %add_rsqrt_fusion.1, bf16[512,7168]{1,0:T(8,128)(2,1)} %concatenate.13, s32[]{:T(128)S(6)} %select_n.119), kind=kOutput, calls=%fused_computation.5 | convolution fusion | flops 4352638976 | bytes 15286276 | tf_op jit(solution)/shard_map/dot_general | solution.py:147
  227.9 10.2 %fusion.5 = f32[512,1184]{0,1:T(8,128)S(1)} fusion(bf16[3584,3552]{1,0:T(8,128)(2,1)} %all-gather.2.cloned.1.call-done, f32[3584]{0:T(1024)S(1)} %copy-done.7, f32[512]{0:T(512)S(1)} %add_rsqrt_fusion.1, bf16[512,7168]{1,0:T(8,128)(2,1)} %concatenate.13, s32[]{:T(128)S(6)} %select_n.119), kind=kOutput, calls=%fused_computation.7 | convolution fusion | flops 4352638976 | bytes 15286276 | tf_op jit(solution)/shard_map/dot_general | solution.py:146
  238.1 15.8 %fusion.10 = bf16[512,3584]{1,0:T(8,128)(2,1)} fusion(bf16[3584,3552]{1,0:T(8,128)(2,1)} %all-gather.2.cloned.1.call-done, f32[512,1184]{0,1:T(8,128)S(1)} %fusion.3, f32[512,1184]{0,1:T(8,128)S(1)} %fusion.5), kind=kOutput, calls=%fused_computation.14 | convolution fusion | flops 4350771200 | bytes 17694720 | tf_op jit(solution)/shard_map/dot_general | solution.py:149
  253.9 49.2 %reduce-scatter.2.cloned.1.call-done = bf16[64,3584]{1,0:T(8,128)(2,1)} async-done(((bf16[512,3584]{1,0:T(8,128)(2,1)}), bf16[64,3584]{1,0:T(8,128)(2,1)}) %reduce-scatter.2.cloned.1.call-update) | async-done | bytes 458768 | tf_op jit(solution)/shard_map/reduce_scatter | solution.py:150
  303.1 2.2 add_convert_fusion
  (52 shorter events, 0.9 us)
Async XLA Ops:
  6.5 10.3 %copy-start = (bf16[160,1280]{1,0:T(8,128)(2,1)S(1)}, bf16[160,1280]{1,0:T(8,128)(2,1)}, u32[]{:S(2)}) copy-start(bf16[160,1280]{1,0:T(8,128)(2,1)} %param.18) | copy-start | bytes 1228804
  6.5 2.5 copy-start.2
  6.5 2.8 copy-start.5
  6.5 3.1 copy-start.8
  6.5 207.0 %all-gather.2.cloned.1.call-start = ((), (), s32[]{:S(2)}) async-start(), calls=%async_computation.4 | async-start | bytes 26492928 | tf_op jit(solution)/shard_map/all_gather | solution.py:43
  18.5 43.9 %all-to-all-start = ((bf16[8,64,1280]{2,1,0:T(8,128)(2,1)}), bf16[8,64,1280]{2,1,0:T(8,128)(2,1)S(1)}, u32[]{:S(2)}, u32[]{:S(2)}) async-start(bf16[8,64,1280]{2,1,0:T(8,128)(2,1)} %bitcast.15), calls=%async_computation | async-start | bytes 2621440 | tf_op jit(solution)/shard_map/all_to_all | solution.py:19
  62.6 4.9 %copy-start.4 = (s32[32,32]{1,0:T(8,128)S(1)}, s32[32,32]{1,0:T(8,128)}, u32[]{:S(2)}) copy-start(s32[32,32]{1,0:T(8,128)} %param.22) | copy-start | bytes 12292
  62.6 5.5 %copy-start.6 = (f32[1280]{0:T(1024)S(1)}, f32[1280]{0:T(1024)}, u32[]{:S(2)}) copy-start(f32[1280]{0:T(1024)} %param.19) | copy-start | bytes 15364
  62.6 5.5 %copy-start.3 = (bf16[384,448]{0,1:T(8,128)(2,1)S(1)}, bf16[384,448]{0,1:T(8,128)(2,1)}, u32[]{:S(2)}) copy-start(bf16[384,448]{0,1:T(8,128)(2,1)} %param.21) | copy-start | bytes 1032196
  63.9 38.3 %all-to-all-start.1 = ((bf16[8,64,1280]{2,1,0:T(8,128)(2,1)}), bf16[8,64,1280]{2,1,0:T(8,128)(2,1)S(1)}, u32[]{:S(2)}, u32[]{:S(2)}) async-start(bf16[8,64,1280]{2,1,0:T(8,128)(2,1)} %broadcast_in_dim.103), calls=%async_computation.1 | async-start | bytes 2621440 | tf_op jit(solution)/shard_map/all_to_all | solution.py:25
  117.6 25.0 %all-to-all-start.2 = ((bf16[32,32,448]{2,1,0:T(8,128)(2,1)}), bf16[32,32,448]{2,1,0:T(8,128)(2,1)S(1)}, u32[]{:S(2)}, u32[]{:S(2)}) async-start(bf16[32,32,448]{2,1,0:T(8,128)(2,1)} %select_select_fusion), calls=%async_computation.2 | async-start | bytes 2097152 | tf_op jit(solution)/shard_map/all_to_all | solution.py:119
  125.5 177.7 %reduce-scatter.2.cloned.1.call-start = ((), (), s32[]{:S(2)}) async-start(), calls=%async_computation.5 | async-start | bytes 4128768 | tf_op jit(solution)/shard_map/reduce_scatter | solution.py:150
  144.8 14.4 %collective-permute-start = (bf16[512,448]{1,0:T(8,128)(2,1)S(1)}, bf16[512,448]{1,0:T(8,128)(2,1)S(1)}, u32[]{:S(2)}, u32[]{:S(2)}) collective-permute-start(bf16[512,448]{1,0:T(8,128)(2,1)S(1)} %broadcast_select_fusion), channel_id=1, source_target_pairs={{0,1},{1,2},{2,3},{3,4},{4,5},{5,6},{6,7},{7,0},{8,9},{9,10},{10,1... | collective-permute-start | bytes 1376264 | tf_op jit(solution)/shard_map/ppermute | solution.py:137
  145.1 14.0 %collective-permute-start.4 = (bf16[512,448]{1,0:T(8,128)(2,1)S(1)}, bf16[512,448]{1,0:T(8,128)(2,1)S(1)}, u32[]{:S(2)}, u32[]{:S(2)}) collective-permute-start(bf16[512,448]{1,0:T(8,128)(2,1)S(1)} %broadcast_select_fusion), channel_id=1, source_target_pairs={{0,7},{1,0},{2,1},{3,2},{4,3},{5,4},{6,5},{7,6},{8,15},{9,8},{10,9... | collective-permute-start | bytes 1376264 | tf_op jit(solution)/shard_map/ppermute | solution.py:139
  159.2 13.4 %collective-permute-start.1 = (bf16[512,448]{1,0:T(8,128)(2,1)S(1)}, bf16[512,448]{1,0:T(8,128)(2,1)S(1)}, u32[]{:S(2)}, u32[]{:S(2)}) collective-permute-start(bf16[512,448]{1,0:T(8,128)(2,1)S(1)} %collective-permute-done), channel_id=1, source_target_pairs={{0,1},{1,2},{2,3},{3,4},{4,5},{5,6},{6,7},{7,0},{8,9},{9,10},{10,1... | collective-permute-start | bytes 1376264 | tf_op jit(solution)/shard_map/ppermute | solution.py:137
  159.2 13.4 %collective-permute-start.5 = (bf16[512,448]{1,0:T(8,128)(2,1)S(1)}, bf16[512,448]{1,0:T(8,128)(2,1)S(1)}, u32[]{:S(2)}, u32[]{:S(2)}) collective-permute-start(bf16[512,448]{1,0:T(8,128)(2,1)S(1)} %collective-permute-done.4), channel_id=1, source_target_pairs={{0,7},{1,0},{2,1},{3,2},{4,3},{5,4},{6,5},{7,6},{8,15},{9,8},{10,9... | collective-permute-start | bytes 1376264 | tf_op jit(solution)/shard_map/ppermute | solution.py:139
  172.6 12.5 %collective-permute-start.2 = (bf16[512,448]{1,0:T(8,128)(2,1)S(1)}, bf16[512,448]{1,0:T(8,128)(2,1)S(1)}, u32[]{:S(2)}, u32[]{:S(2)}) collective-permute-start(bf16[512,448]{1,0:T(8,128)(2,1)S(1)} %collective-permute-done.1), channel_id=1, source_target_pairs={{0,1},{1,2},{2,3},{3,4},{4,5},{5,6},{6,7},{7,0},{8,9},{9,10},{10,1... | collective-permute-start | bytes 1376264 | tf_op jit(solution)/shard_map/ppermute | solution.py:137
  172.6 12.5 %collective-permute-start.6 = (bf16[512,448]{1,0:T(8,128)(2,1)S(1)}, bf16[512,448]{1,0:T(8,128)(2,1)}, u32[]{:S(2)}, u32[]{:S(2)}) collective-permute-start(bf16[512,448]{1,0:T(8,128)(2,1)S(1)} %collective-permute-done.5), channel_id=1, source_target_pairs={{0,7},{1,0},{2,1},{3,2},{4,3},{5,4},{6,5},{7,6},{8,15},{9,8},{10,9... | collective-permute-start | bytes 1376264 | tf_op jit(solution)/shard_map/ppermute | solution.py:139
  185.1 11.7 %collective-permute-start.3 = (bf16[512,448]{1,0:T(8,128)(2,1)S(1)}, bf16[512,448]{1,0:T(8,128)(2,1)}, u32[]{:S(2)}, u32[]{:S(2)}) collective-permute-start(bf16[512,448]{1,0:T(8,128)(2,1)S(1)} %collective-permute-done.2), channel_id=1, source_target_pairs={{0,1},{1,2},{2,3},{3,4},{4,5},{5,6},{6,7},{7,0},{8,9},{9,10},{10,1... | collective-permute-start | bytes 1376264 | tf_op jit(solution)/shard_map/ppermute | solution.py:137
  208.3 5.3 %copy-start.7 = (f32[3584]{0:T(1024)S(1)}, f32[3584]{0:T(1024)}, u32[]{:S(2)}) copy-start(f32[3584]{0:T(1024)} %param.24) | copy-start | bytes 43012
  238.1 67.3 %copy-start.1 = (bf16[160,1280]{1,0:T(8,128)(2,1)S(1)}, bf16[160,1280]{1,0:T(8,128)(2,1)}, u32[]{:S(2)}) copy-start(bf16[160,1280]{1,0:T(8,128)(2,1)} %param.18) | copy-start | bytes 1228804
Sparse Core Ops, SparseCore 0:
  9.9 102.6 all-gather.1
  254.1 49.0 reduce-scatter.1
